TPU v7x, 32 devices: a whole 2x2x4 slice. The times are simulated.
32 devices in a mesh: row: 4 (over z), col: 8 (over y, x, core).
Axes of the slice: x: 2, y: 2, z: 4, core: 2. Of those that a mesh axis runs over, the one named last changes fastest.
Arguments:
- hamiltonian: bfloat16 [2048, 2048], P('row', 'col'), may hold values from -0.3 to 0.3
- pattern: int32 [16, 16], replicated, may hold values from 0 to 1, as said below
- tile_lists: int32 [32, 8], replicated, may hold values from 0 to 15, as said below
- orders: int32 [32], replicated, may hold values from 6 to 8
- shift: float32 [1], replicated, may hold values from -0.5 to 0.5
Outputs:
- density: bfloat16 [2048, 2048], P('row', 'col')
- php: float32 [2048, 2048], P('row', 'col')
Inputs may be any that keep to these rules, and one draw needn't show every extreme that they name: `pattern`: Symmetric, with zeros on the diagonal. `tile_lists`: row s begins with tile s * 64 // 128; its entries lie in distinct groups of 2 consecutive tiles, and the second lies in the group that shares a group of 4 consecutive tiles with the first. Entries from position orders[s] on are not used.
All inputs are finite; a program needn't handle non-finite values.
Results may differ from a plain program's by a relative error of at most 0.0073.
Values may be sent and summed in bfloat16 or wider, within the bound.
A program may use at most 64 MiB of HBM per device.

v0:
```python
import jax
import jax.numpy as jnp
from jax import lax
from jax.sharding import PartitionSpec as P

TILE = 128
TPC = 2
MAXT = 8
ITERS = 3


def newton_density(sub, live_rows, potential):
    eye = jnp.eye(sub.shape[0], dtype=jnp.float32)
    shifted = sub.astype(jnp.float32) - potential * eye * live_rows[None, :]
    row_squares = jnp.sum(shifted * shifted, axis=1)
    scale = jnp.abs(potential) + 2.0 * jnp.sqrt(jnp.max(row_squares) + 1e-06)
    iterate = (shifted / scale).astype(jnp.bfloat16)
    product = shifted
    for step in range(ITERS):
        square = jnp.dot(iterate, iterate, preferred_element_type=jnp.float32)
        factor = (1.5 * eye - 0.5 * square).astype(jnp.bfloat16)
        product = jnp.dot(iterate, factor, preferred_element_type=jnp.float32)
        if step + 1 < ITERS:
            iterate = product.astype(jnp.bfloat16)
    return 0.5 * (eye - product)


def per_device(hamiltonian, pattern, tile_lists, orders, shift):
    rows_n = lax.axis_size("row")
    cols_n = lax.axis_size("col")
    devices = rows_n * cols_n
    me_row = lax.axis_index("row")
    me_col = lax.axis_index("col")
    solver = me_row * cols_n + me_col
    count = pattern.shape[0]
    row_tiles = count // rows_n
    width = TPC * TILE // rows_n
    pairs = MAXT * MAXT
    steps = jnp.arange(MAXT, dtype=jnp.int32)
    keep = jnp.maximum(pattern, jnp.eye(count, dtype=jnp.int32))
    local_keep = lax.dynamic_slice(keep, (me_row * row_tiles, me_col * TPC), (row_tiles, TPC))
    full_keep = jnp.repeat(jnp.repeat(local_keep, TILE, axis=0), TILE, axis=1)
    masked = jnp.where(full_keep > 0, hamiltonian, jnp.zeros_like(hamiltonian))
    blocks = (
        masked.reshape(row_tiles, TILE, TPC, TILE)
        .transpose(0, 2, 1, 3)
        .reshape(row_tiles * TPC, TILE, TILE)
    )
    live_all = steps[None, :] < orders[:, None]
    owned = (tile_lists[:, :, None] // row_tiles == me_row) & (
        tile_lists[:, None, :] // TPC == me_col
    )
    owned = owned & live_all[:, :, None] & live_all[:, None, :]
    owned = owned.reshape(devices, pairs)
    rank = jnp.cumsum(owned.astype(jnp.int32), axis=1) - 1
    local_index = (
        (tile_lists[:, :, None] - me_row * row_tiles) * TPC
        + (tile_lists[:, None, :] - me_col * TPC)
    ).reshape(devices, pairs)
    slots = []
    for slot in range(2):
        pick = owned & (rank == slot)
        found = jnp.any(pick, axis=1)
        which = jnp.sum(jnp.where(pick, local_index, 0), axis=1)
        picked = jnp.take(blocks, which, axis=0)
        slots.append(jnp.where(found[:, None, None], picked, jnp.zeros_like(picked)))
    outgoing = jnp.stack(slots, axis=1)
    arrived = lax.all_to_all(outgoing, ("row", "col"), split_axis=0, concat_axis=0, tiled=True)
    arrived = arrived.reshape(devices * 2, TILE, TILE)
    mine = lax.dynamic_index_in_dim(tile_lists, solver, 0, keepdims=False)
    order_here = lax.dynamic_index_in_dim(orders, solver, 0, keepdims=False)
    live = steps < order_here
    both = (live[:, None] & live[None, :]).reshape(pairs)
    owner = (mine[:, None] // row_tiles * cols_n + mine[None, :] // TPC).reshape(pairs)
    flat_pairs = jnp.arange(pairs, dtype=jnp.int32)
    earlier = (
        (owner[:, None] == owner[None, :])
        & both[None, :]
        & (flat_pairs[None, :] < flat_pairs[:, None])
    )
    slot_of = jnp.sum(earlier.astype(jnp.int32), axis=1)
    source = jnp.where(both, owner * 2 + slot_of, 0)
    sub = jnp.take(arrived, source, axis=0)
    sub = jnp.where(both[:, None, None], sub, jnp.zeros_like(sub))
    sub = (
        sub.reshape(MAXT, MAXT, TILE, TILE).transpose(0, 2, 1, 3).reshape(MAXT * TILE, MAXT * TILE)
    )
    live_rows = jnp.repeat(live.astype(jnp.float32), TILE)
    dens = newton_density(sub, live_rows, shift[0])
    offset = solver * width % TILE
    central = lax.dynamic_slice_in_dim(dens, offset, width, 1).astype(jnp.bfloat16)
    central = central.reshape(MAXT, TILE, width).transpose(0, 2, 1)
    home_col = solver * width // (TPC * TILE)
    groups = mine // row_tiles
    ahead = (groups[:, None] == groups[None, :]) & live[None, :] & (steps[None, :] < steps[:, None])
    place = jnp.sum(ahead.astype(jnp.int32), axis=1)
    target = groups * cols_n + home_col
    chooser = jnp.arange(devices, dtype=jnp.int32)[:, None, None] == target[None, None, :]
    chooser = (
        chooser
        & (jnp.arange(2, dtype=jnp.int32)[None, :, None] == place[None, None, :])
        & live[None, None, :]
    )
    back = jnp.einsum(
        "dki,iwt->dkwt", chooser.astype(jnp.bfloat16), central, preferred_element_type=jnp.float32
    ).astype(jnp.bfloat16)
    returned = lax.all_to_all(back, ("row", "col"), split_axis=0, concat_axis=0, tiled=True)
    returned = returned.reshape(devices * 2, width, TILE)
    homes = lax.dynamic_slice_in_dim(tile_lists, me_col * rows_n, rows_n, 0)
    home_orders = lax.dynamic_slice_in_dim(orders, me_col * rows_n, rows_n, 0)
    home_live = steps[None, :] < home_orders[:, None]
    home_groups = homes // row_tiles
    home_ahead = (
        (home_groups[:, :, None] == home_groups[:, None, :])
        & home_live[:, None, :]
        & (steps[None, None, :] < steps[None, :, None])
    )
    home_place = jnp.sum(home_ahead.astype(jnp.int32), axis=2)
    local_rows = me_row * row_tiles + jnp.arange(row_tiles, dtype=jnp.int32)
    hit = (homes[None, :, :] == local_rows[:, None, None]) & home_live[None, :, :]
    found = jnp.any(hit, axis=2)
    slot_here = jnp.sum(jnp.where(hit, home_place[None, :, :], 0), axis=2)
    sub_index = me_col * rows_n + jnp.arange(rows_n, dtype=jnp.int32)
    flat_index = jnp.where(found, sub_index[None, :] * 2 + slot_here, 0)
    pieces = jnp.take(returned, flat_index.reshape(-1), axis=0).reshape(
        row_tiles, rows_n, width, TILE
    )
    pieces = jnp.where(found[:, :, None, None], pieces, jnp.zeros_like(pieces))
    density = pieces.transpose(0, 3, 1, 2).reshape(row_tiles * TILE, rows_n * width)
    p_strip = lax.all_gather(density, "row", axis=0, tiled=True)
    part = p_strip
    hp = jnp.dot(
        lax.all_gather(masked, "col", axis=1, tiled=True), part, preferred_element_type=jnp.float32
    ).astype(jnp.bfloat16)
    q_strip = lax.all_gather(hp, "row", axis=0, tiled=True)
    part = q_strip
    php = jnp.dot(
        lax.all_gather(density, "col", axis=1, tiled=True), part, preferred_element_type=jnp.float32
    )
    return (density, php)


def solution(mesh):
    in_specs = (P("row", "col"), P(), P(), P(), P())
    out_specs = (P("row", "col"), P("row", "col"))
    return jax.shard_map(
        per_device, mesh=mesh, in_specs=in_specs, out_specs=out_specs, check_vma=False
    )
```

profile of v0, /device:TPU:0, one launch (start us, length us, event | category | flops | bytes accessed | tf_op | source)
XLA Modules:
  0.0 244.3 jit_solution(1091136820264881119)
XLA Ops:
  7.2 0.7 fusion.31
  7.9 0.7 subtract_multiply_fusion
  8.6 0.7 iota_compare_fusion.2
  9.3 0.2 reduce_window_sum.11
  10.0 0.8 fusion.42
  11.0 1.1 copy.77
  12.2 0.2 copy.78
  12.4 0.7 gather_fusion.2
  13.2 0.7 gather_fusion.3
  14.1 0.2 fusion.12
  14.6 1.5 copy.81
  16.1 7.3 %all-to-all-start = ((bf16[32,2,128,128]{3,2,1,0:T(8,128)(2,1)}), bf16[32,2,128,128]{3,2,1,0:T(8,128)(2,1)S(1)}, u32[]{:S(2)}, u32[]{:S(2)}) async-start(bf16[32,2,128,128]{3,2,1,0:T(8,128)(2,1)} %copy.81), calls=%async_computation | async-start | bytes 4194304 | tf_op jit(solution)/shard_map/all_to_all | solution.py:68
  23.5 0.7 all-gather.7.cloned.1.call-update
  24.2 0.6 dynamic_slice.23
  24.8 0.6 iota_compare_fusion.7
  25.7 0.2 fusion.27
  27.2 0.7 fusion.55
  27.9 0.3 iota_compare_fusion
  28.5 43.7 %all-to-all-done = bf16[32,2,128,128]{3,2,1,0:T(8,128)(2,1)S(1)} async-done(((bf16[32,2,128,128]{3,2,1,0:T(8,128)(2,1)}), bf16[32,2,128,128]{3,2,1,0:T(8,128)(2,1)S(1)}, u32[]{:S(2)}, u32[]{:S(2)}) %all-to-all-start) | async-done | bytes 2097184 | tf_op jit(solution)/shard_map/all_to_all | solution.py:68
  72.2 1.3 copy-done.1
  73.5 2.5 %gather_fusion = bf16[64,128,128]{2,1,0:T(8,128)(2,1)S(1)} fusion(bf16[64,128,128]{2,1,0:T(8,128)(2,1)} %bitcast.105, s32[1024]{0:T(1024)S(1)} %pad_clamp_fusion.1), kind=kCustom, calls=%fused_computation.2 | custom fusion | bytes 4194560 | tf_op jit(solution)/shard_map/jit(_take)/gather | solution.py:83
  76.1 2.4 convert_bitcast_fusion
  78.5 1.7 multiply_reduce_fusion
  80.2 0.6 reduce_max.9
  81.5 1.8 divide_convert_fusion
  83.3 1.4 copy.83
  84.7 4.3 %copy.82 = f32[8,128,8,128]{3,2,1,0:T(8,128)} copy(f32[8,128,8,128]{3,1,2,0:T(8,128)S(1)} %copy-done) | data formatting | bytes 8388608 | tf_op jit(solution)/shard_map/convert_element_type | solution.py:14
  89.0 8.2 %fusion.9 = bf16[1024,1024]{1,0:T(8,128)(2,1)} fusion(f32[128,8,8,128]{3,2,1,0:T(8,128)} %bitcast.106, f32[]{:T(128)S(6)} %add.284, f32[1024]{0:T(1024)S(1)} %broadcast_bitcast_fusion, f32[]{:T(128)} %bitcast.98, bf16[128,8,8,128]{3,2,1,0:T(8,128)(2,1)S(1)} %bitcast.110), kind=kOutput, calls=%fused_computation.23 | convolution fusion | flops 4307550208 | bytes 8392712 | tf_op jit(solution)/shard_map/dot_general | solution.py:22
  97.1 7.5 %convolution_convert_fusion = bf16[1024,1024]{1,0:T(8,128)(2,1)S(1)} fusion(bf16[1024,1024]{1,0:T(8,128)(2,1)} %fusion.9), kind=kOutput, calls=%fused_computation.24 | convolution fusion | flops 4301258752 | bytes 4194304 | tf_op jit(solution)/shard_map/dot_general | solution.py:22
  104.7 6.6 %fusion.16 = f32[1024,1024]{1,0:T(8,128)} fusion(bf16[1024,1024]{1,0:T(8,128)(2,1)S(1)} %convolution_convert_fusion), kind=kOutput, calls=%fused_computation.31 | convolution fusion | flops 4300210176 | bytes 6291456 | tf_op jit(solution)/shard_map/dot_general | solution.py:22
  111.3 1.4 fusion.18
  112.9 0.5 convolution_convert_fusion.1
  113.4 1.4 copy.86
  114.8 4.1 %all-to-all-start.1 = ((bf16[32,2,64,128]{3,2,1,0:T(8,128)(2,1)}), bf16[32,2,64,128]{3,2,1,0:T(8,128)(2,1)S(1)}, u32[]{:S(2)}, u32[]{:S(2)}) async-start(bf16[32,2,64,128]{3,2,1,0:T(8,128)(2,1)} %copy.86), calls=%async_computation.1 | async-start | bytes 2097152 | tf_op jit(solution)/shard_map/all_to_all | solution.py:107
  119.4 0.2 fusion.24
  119.6 0.2 convert_reduce_fusion.1
  119.8 0.2 select_reduce_fusion.2
  120.2 25.0 %all-to-all-done.1 = bf16[32,2,64,128]{3,2,1,0:T(8,128)(2,1)S(1)} async-done(((bf16[32,2,64,128]{3,2,1,0:T(8,128)(2,1)}), bf16[32,2,64,128]{3,2,1,0:T(8,128)(2,1)S(1)}, u32[]{:S(2)}, u32[]{:S(2)}) %all-to-all-start.1) | async-done | bytes 1048608 | tf_op jit(solution)/shard_map/all_to_all | solution.py:107
  145.1 0.6 gather_fusion.1
  145.8 0.2 copy.87
  146.1 0.7 copy.107
  146.9 27.1 %all-gather.9.cloned.1.call-done = bf16[2048,256]{0,1:T(8,128)(2,1)} async-done(((bf16[512,256]{0,1:T(8,128)(2,1)}), bf16[2048,256]{0,1:T(8,128)(2,1)}) %all-gather.9.cloned.1.call-update) | async-done | bytes 1048592 | tf_op jit(solution)/shard_map/all_gather | solution.py:130
  174.0 3.3 %convolution_convert_fusion.2 = bf16[512,256]{1,0:T(8,128)(2,1)} fusion(bf16[512,2048]{0,1:T(8,128)(2,1)} %all-gather.7.cloned.1.call-done, bf16[2048,256]{0,1:T(8,128)(2,1)} %all-gather.9.cloned.1.call-done), kind=kOutput, calls=%fused_computation.26 | convolution fusion | flops 537001984 | bytes 3407872 | tf_op jit(solution)/shard_map/dot_general | solution.py:132
  177.4 0.5 all-gather.5.cloned.1.call-update
  177.9 0.8 copy.88
  178.8 26.1 %all-gather.11.cloned.1.call-done = bf16[2048,256]{1,0:T(8,128)(2,1)} async-done(((bf16[512,256]{1,0:T(8,128)(2,1)}), bf16[2048,256]{1,0:T(8,128)(2,1)}) %all-gather.11.cloned.1.call-update) | async-done | bytes 1048592 | tf_op jit(solution)/shard_map/all_gather | solution.py:135
  204.8 29.5 %all-gather.5.cloned.1.call-done = bf16[512,2048]{0,1:T(8,128)(2,1)} async-done(((bf16[512,256]{0,1:T(8,128)(2,1)}), bf16[512,2048]{0,1:T(8,128)(2,1)}) %all-gather.5.cloned.1.call-update) | async-done | bytes 2097168 | tf_op jit(solution)/shard_map/all_gather | solution.py:138
  234.3 3.4 %fusion.59 = f32[512,256]{1,0:T(8,128)} fusion(bf16[512,2048]{0,1:T(8,128)(2,1)} %all-gather.5.cloned.1.call-done, bf16[2048,256]{1,0:T(8,128)(2,1)} %all-gather.11.cloned.1.call-done), kind=kOutput, calls=%fused_computation.154 | convolution fusion | flops 536870912 | bytes 3670016 | tf_op jit(solution)/shard_map/dot_general | solution.py:137
  (67 shorter events, 3.3 us)
Async XLA Ops:
  12.1 2.3 copy-start.3
  14.6 9.6 %copy-start.5 = (s32[32]{0:T(128)S(1)}, s32[32]{0:T(128)}, u32[]{:S(2)}) copy-start(s32[32]{0:T(128)} %param.10) | copy-start | bytes 388
  14.6 11.1 %copy-start.4 = (s32[32,8]{0,1:T(8,128)S(1)}, s32[32,8]{0,1:T(8,128)}, u32[]{:S(2)}) copy-start(s32[32,8]{0,1:T(8,128)} %param.9) | copy-start | bytes 3076
  16.1 56.1 %all-to-all-start = ((bf16[32,2,128,128]{3,2,1,0:T(8,128)(2,1)}), bf16[32,2,128,128]{3,2,1,0:T(8,128)(2,1)S(1)}, u32[]{:S(2)}, u32[]{:S(2)}) async-start(bf16[32,2,128,128]{3,2,1,0:T(8,128)(2,1)} %copy.81), calls=%async_computation | async-start | bytes 4194304 | tf_op jit(solution)/shard_map/all_to_all | solution.py:68
  23.4 123.5 %all-gather.7.cloned.1.call-start = ((), (), s32[]{:S(2)}) async-start(), calls=%async_computation.3 | async-start | bytes 2359296 | tf_op jit(solution)/shard_map/all_gather | solution.py:133
  72.2 1.4 copy-start.1
  81.5 3.2 %copy-start = (f32[8,128,8,128]{3,1,2,0:T(8,128)S(1)}, f32[8,128,8,128]{3,1,2,0:T(8,128)}, u32[]{:S(2)}) copy-start(f32[8,128,8,128]{3,1,2,0:T(8,128)} %convert_bitcast_fusion) | copy-start | bytes 12582916
  114.8 30.3 %all-to-all-start.1 = ((bf16[32,2,64,128]{3,2,1,0:T(8,128)(2,1)}), bf16[32,2,64,128]{3,2,1,0:T(8,128)(2,1)S(1)}, u32[]{:S(2)}, u32[]{:S(2)}) async-start(bf16[32,2,64,128]{3,2,1,0:T(8,128)(2,1)} %copy.86), calls=%async_computation.1 | async-start | bytes 2097152 | tf_op jit(solution)/shard_map/all_to_all | solution.py:107
  118.9 55.1 %all-gather.9.cloned.1.call-start = ((), (), s32[]{:S(2)}) async-start(), calls=%async_computation.4 | async-start | bytes 1310720 | tf_op jit(solution)/shard_map/all_gather | solution.py:130
  146.8 31.1 %copy-start.2 = (bf16[32,8,4,128]{3,1,2,0:T(8,128)(2,1)S(1)}, bf16[32,8,4,128]{3,1,2,0:T(8,128)(2,1)}, u32[]{:S(2)}) copy-start(bf16[32,8,4,128]{3,1,2,0:T(8,128)(2,1)} %copy.107) | copy-start | bytes 786436
  146.8 58.0 %all-gather.11.cloned.1.call-start = ((), (), s32[]{:S(2)}) async-start(), calls=%async_computation.5 | async-start | bytes 1310720 | tf_op jit(solution)/shard_map/all_gather | solution.py:135
  177.3 57.0 %all-gather.5.cloned.1.call-start = ((), (), s32[]{:S(2)}) async-start(), calls=%async_computation.2 | async-start | bytes 2359296 | tf_op jit(solution)/shard_map/all_gather | solution.py:138
Sparse Core Ops, SparseCore 0:
  26.7 35.3 all-gather.6
  146.9 26.9 all-gather.8
  177.5 27.3 all-gather.10
  207.2 27.1 all-gather.4
where the time goes:
time: 245 us; the launch traced here: 244 us
  waiting for transfers between devices  153 us (62%)
  matrix products  29.6 us (12%)
  local copies, waits for them, and re-layouts  19.7 us (8%)
  between operations  15.6 us (6%)
  other arithmetic  15.3 us (6%)
  starting transfers between devices  11.6 us (5%)
    all_to_all x1, waiting for transfers between devices, per_device(): lax.all_to_all(outgoing, ('row', 'col'), split_axis=0, concat_axis=0, til...  43.7 us
    all_gather x1, waiting for transfers between devices, per_device(): lax.all_gather(density, 'col', axis=1, tiled=True)  29.5 us
    all_gather x1, waiting for transfers between devices, per_device(): p_strip = lax.all_gather(density, 'row', axis=0, tiled=True)  27.1 us
    all_gather x1, waiting for transfers between devices, per_device(): q_strip = lax.all_gather(hp, 'row', axis=0, tiled=True)  26.1 us
    all_to_all x1, waiting for transfers between devices, per_device(): lax.all_to_all(back, ('row', 'col'), split_axis=0, concat_axis=0, tiled=T...  25 us
    dot_general x3, matrix products, newton_density(): product = jnp.dot(iterate, factor, preferred_element_type=jnp.float32)  22.3 us
    all_to_all x1, starting transfers between devices, per_device(): lax.all_to_all(outgoing, ('row', 'col'), split_axis=0, concat_axis=0, til...  7.33 us
  transfers between devices with their start and end apart: 6, of which 5 were waited for; matrix products, arithmetic and copies ran while one was open for 20% of the time, Pallas kernels for 0%

commit v1 on v0

--- a/solution.py
+++ b/solution.py
@@ -7,6 +7,16 @@
 TPC = 2
 MAXT = 8
 ITERS = 3
+
+
+def gather_by_hops(x, mesh_axis, dim):
+    size = lax.axis_size(mesh_axis)
+    moving, blocks = (x, [x])
+    for _ in range(size - 1):
+        moving = lax.ppermute(moving, mesh_axis, [(i, (i + 1) % size) for i in range(size)])
+        blocks.insert(0, moving)
+    merged = jnp.concatenate(blocks, axis=dim)
+    return jnp.roll(merged, (lax.axis_index(mesh_axis) + 1) * x.shape[dim], axis=dim)
 
 
 def newton_density(sub, live_rows, potential):
@@ -132,7 +142,7 @@
     hp = jnp.dot(
         lax.all_gather(masked, "col", axis=1, tiled=True), part, preferred_element_type=jnp.float32
     ).astype(jnp.bfloat16)
-    q_strip = lax.all_gather(hp, "row", axis=0, tiled=True)
+    q_strip = gather_by_hops(hp, "row", 0)
     part = q_strip
     php = jnp.dot(
         lax.all_gather(density, "col", axis=1, tiled=True), part, preferred_element_type=jnp.float32

time: 245 us -> 220 us (0.90)
  waiting for transfers between devices: 153 us -> 120 us
  local copies, waits for them, and re-layouts: 19.7 us -> 26.4 us
    all_gather x1, waiting for transfers between devices: 29.5 us -> 0.01 us  [per_device(): lax.all_gather(density, 'col', axis=1, tiled=True)]
    all_gather x1 -> x0, waiting for transfers between devices: 26.1 us -> none  [per_device(): q_strip = lax.all_gather(hp, 'row', axis=0, tiled=True)]
    ppermute x0 -> x3, waiting for transfers between devices: none -> 23.8 us  [gather_by_hops(): lax.ppermute(moving, mesh_axis, [(i, (i + 1) % size) for i in range(size)])]
    unnamed x17 -> x24, local copies, waits for them, and re-layouts: 4.14 us -> 10 us
  transfers between devices with their start and end apart: 6 -> 8, of which waited for: 5 -> 6; matrix products, arithmetic and copies ran while one was open for 20% -> 26% of each run, Pallas kernels for 0% -> 0%
where the time goes in v1:
time: 220 us; the launch traced here: 219 us
  waiting for transfers between devices  120 us (55%)
  matrix products  28.9 us (13%)
  local copies, waits for them, and re-layouts  26.4 us (12%)
  between operations  15.5 us (7%)
  other arithmetic  15.3 us (7%)
  starting transfers between devices  13.1 us (6%)
    all_to_all x1, waiting for transfers between devices, per_device(): lax.all_to_all(outgoing, ('row', 'col'), split_axis=0, concat_axis=0, til...  43.7 us
    all_gather x1, waiting for transfers between devices, per_device(): p_strip = lax.all_gather(density, 'row', axis=0, tiled=True)  26.4 us
    all_to_all x1, waiting for transfers between devices, per_device(): lax.all_to_all(back, ('row', 'col'), split_axis=0, concat_axis=0, tiled=T...  25 us
    ppermute x3, waiting for transfers between devices, gather_by_hops(): lax.ppermute(moving, mesh_axis, [(i, (i + 1) % size) for i in range(size)])  23.8 us
    dot_general x3, matrix products, newton_density(): product = jnp.dot(iterate, factor, preferred_element_type=jnp.float32)  22.3 us
    unnamed x24, local copies, waits for them, and re-layouts  10 us
    all_to_all x1, starting transfers between devices, per_device(): lax.all_to_all(outgoing, ('row', 'col'), split_axis=0, concat_axis=0, til...  7.33 us
  transfers between devices with their start and end apart: 8, of which 6 were waited for; matrix products, arithmetic and copies ran while one was open for 26% of the time, Pallas kernels for 0%

profile of v1, /device:TPU:0, one launch (start us, length us, event | category | flops | bytes accessed | tf_op | source)
XLA Modules:
  0.0 219.3 jit_solution(7619980431018422989)
XLA Ops:
  7.2 0.7 fusion.33
  7.9 0.7 subtract_multiply_fusion
  8.6 0.7 iota_compare_fusion.2
  10.0 0.8 fusion.44
  11.0 1.1 copy.77
  12.4 0.7 gather_fusion.2
  13.2 0.7 gather_fusion.3
  14.6 1.6 copy.81
  16.2 7.3 %all-to-all-start = ((bf16[32,2,128,128]{3,2,1,0:T(8,128)(2,1)}), bf16[32,2,128,128]{3,2,1,0:T(8,128)(2,1)S(1)}, u32[]{:S(2)}, u32[]{:S(2)}) async-start(bf16[32,2,128,128]{3,2,1,0:T(8,128)(2,1)} %copy.81), calls=%async_computation | async-start | bytes 4194304 | tf_op jit(solution)/shard_map/all_to_all | solution.py:78
  23.6 0.7 all-gather.6.cloned.1.call-update
  24.9 0.6 iota_compare_fusion.7
  27.3 0.7 fusion.58
  28.6 43.7 %all-to-all-done = bf16[32,2,128,128]{3,2,1,0:T(8,128)(2,1)S(1)} async-done(((bf16[32,2,128,128]{3,2,1,0:T(8,128)(2,1)}), bf16[32,2,128,128]{3,2,1,0:T(8,128)(2,1)S(1)}, u32[]{:S(2)}, u32[]{:S(2)}) %all-to-all-start) | async-done | bytes 2097184 | tf_op jit(solution)/shard_map/all_to_all | solution.py:78
  72.3 1.3 copy-done.1
  73.6 2.5 %gather_fusion = bf16[64,128,128]{2,1,0:T(8,128)(2,1)S(1)} fusion(bf16[64,128,128]{2,1,0:T(8,128)(2,1)} %bitcast.104, s32[1024]{0:T(1024)S(1)} %pad_clamp_fusion.1), kind=kCustom, calls=%fused_computation.2 | custom fusion | bytes 4194560 | tf_op jit(solution)/shard_map/jit(_take)/gather | solution.py:93
  76.2 2.4 %convert_bitcast_fusion = f32[8,128,8,128]{3,1,2,0:T(8,128)} fusion(pred[8,8]{1,0:T(8,128)(4,1)S(1)} %compare_and_fusion.3, pred[8,8]{1,0:T(8,128)(4,1)S(1)} %broadcast_and_fusion, bf16[64,128,128]{2,1,0:T(8,128)(2,1)S(1)} %gather_fusion), kind=kLoop, calls=%fused_computation.13 | loop fusion | flops 3145728 | bytes 6291584 | tf_op jit(solution)/shard_map/convert_element_type | solution.py:24
  78.5 1.7 multiply_reduce_fusion
  80.3 0.6 reduce_max.9
  81.6 1.8 divide_convert_fusion
  83.4 1.4 copy.83
  84.7 0.8 copy-done
  85.6 4.3 %copy.82 = f32[8,128,8,128]{3,2,1,0:T(8,128)} copy(f32[8,128,8,128]{3,1,2,0:T(8,128)S(1)} %copy-done) | data formatting | bytes 8388608 | tf_op jit(solution)/shard_map/convert_element_type | solution.py:24
  89.9 8.2 %fusion.9 = bf16[1024,1024]{1,0:T(8,128)(2,1)} fusion(f32[128,8,8,128]{3,2,1,0:T(8,128)} %bitcast.105, f32[]{:T(128)S(6)} %add.297, f32[1024]{0:T(1024)S(1)} %broadcast_bitcast_fusion, f32[]{:T(128)} %bitcast.97, bf16[128,8,8,128]{3,2,1,0:T(8,128)(2,1)S(1)} %bitcast.109), kind=kOutput, calls=%fused_computation.23 | convolution fusion | flops 4307550208 | bytes 8392712 | tf_op jit(solution)/shard_map/dot_general | solution.py:32
  98.0 7.5 %convolution_convert_fusion = bf16[1024,1024]{1,0:T(8,128)(2,1)S(1)} fusion(bf16[1024,1024]{1,0:T(8,128)(2,1)} %fusion.9), kind=kOutput, calls=%fused_computation.24 | convolution fusion | flops 4301258752 | bytes 4194304 | tf_op jit(solution)/shard_map/dot_general | solution.py:32
  105.6 6.6 %fusion.18 = f32[1024,1024]{1,0:T(8,128)} fusion(bf16[1024,1024]{1,0:T(8,128)(2,1)S(1)} %convolution_convert_fusion), kind=kOutput, calls=%fused_computation.33 | convolution fusion | flops 4300210176 | bytes 6291456 | tf_op jit(solution)/shard_map/dot_general | solution.py:32
  112.2 1.4 fusion.20
  114.3 1.4 copy.86
  115.7 4.1 %all-to-all-start.1 = ((bf16[32,2,64,128]{3,2,1,0:T(8,128)(2,1)}), bf16[32,2,64,128]{3,2,1,0:T(8,128)(2,1)S(1)}, u32[]{:S(2)}, u32[]{:S(2)}) async-start(bf16[32,2,64,128]{3,2,1,0:T(8,128)(2,1)} %copy.86), calls=%async_computation.1 | async-start | bytes 2097152 | tf_op jit(solution)/shard_map/all_to_all | solution.py:117
  121.0 25.0 %all-to-all-done.1 = bf16[32,2,64,128]{3,2,1,0:T(8,128)(2,1)S(1)} async-done(((bf16[32,2,64,128]{3,2,1,0:T(8,128)(2,1)}), bf16[32,2,64,128]{3,2,1,0:T(8,128)(2,1)S(1)}, u32[]{:S(2)}, u32[]{:S(2)}) %all-to-all-start.1) | async-done | bytes 1048608 | tf_op jit(solution)/shard_map/all_to_all | solution.py:117
  146.0 0.6 gather_fusion.1
  146.9 0.7 copy.107
  147.8 0.7 all-gather.4.cloned.1.call-update
  148.5 26.4 %all-gather.8.cloned.1.call-done = bf16[2048,256]{0,1:T(8,128)(2,1)} async-done(((bf16[512,256]{0,1:T(8,128)(2,1)}), bf16[2048,256]{0,1:T(8,128)(2,1)}) %all-gather.8.cloned.1.call-update) | async-done | bytes 1048592 | tf_op jit(solution)/shard_map/all_gather | solution.py:140
  174.9 2.6 %convolution_convert_fusion.2 = bf16[512,256]{1,0:T(8,128)(2,1)S(1)} fusion(bf16[512,2048]{0,1:T(8,128)(2,1)} %all-gather.6.cloned.1.call-done, bf16[2048,256]{0,1:T(8,128)(2,1)} %all-gather.8.cloned.1.call-done), kind=kOutput, calls=%fused_computation.26 | convolution fusion | flops 537001984 | bytes 3407872 | tf_op jit(solution)/shard_map/dot_general | solution.py:142
  177.5 1.5 collective-permute-start
  179.0 7.9 %collective-permute-done = bf16[512,256]{1,0:T(8,128)(2,1)S(1)} collective-permute-done((bf16[512,256]{1,0:T(8,128)(2,1)S(1)}, bf16[512,256]{1,0:T(8,128)(2,1)S(1)}, u32[]{:S(2)}, u32[]{:S(2)}) %collective-permute-start) | collective-permute-done | bytes 262176 | tf_op jit(solution)/shard_map/ppermute | solution.py:16
  186.9 8.5 %collective-permute-done.1 = bf16[512,256]{1,0:T(8,128)(2,1)S(1)} collective-permute-done((bf16[512,256]{1,0:T(8,128)(2,1)S(1)}, bf16[512,256]{1,0:T(8,128)(2,1)S(1)}, u32[]{:S(2)}, u32[]{:S(2)}) %collective-permute-start.1) | collective-permute-done | bytes 262176 | tf_op jit(solution)/shard_map/ppermute | solution.py:16
  195.4 0.8 copy.88
  196.3 7.3 %collective-permute-done.2 = bf16[512,256]{1,0:T(8,128)(2,1)S(1)} collective-permute-done((bf16[512,256]{1,0:T(8,128)(2,1)S(1)}, bf16[512,256]{1,0:T(8,128)(2,1)S(1)}, u32[]{:S(2)}, u32[]{:S(2)}) %collective-permute-start.2) | collective-permute-done | bytes 262176 | tf_op jit(solution)/shard_map/ppermute | solution.py:16
  203.6 0.7 constant_dynamic-update-slice_fusion.7
  204.3 0.7 constant_dynamic-update-slice_fusion.6
  205.0 0.7 constant_dynamic-update-slice_fusion.5
  205.8 0.7 constant_dynamic-update-slice_fusion.4
  206.5 0.7 constant_dynamic-update-slice_fusion.3
  207.2 0.7 constant_dynamic-update-slice_fusion.2
  208.0 0.7 constant_dynamic-update-slice_fusion.1
  208.7 0.7 constant_dynamic-update-slice_fusion
  209.4 3.4 %fusion.14 = f32[512,256]{1,0:T(8,128)} fusion(bf16[512,2048]{0,1:T(8,128)(2,1)} %all-gather.4.cloned.1.call-done, bf16[4096,256]{1,0:T(8,128)(2,1)} %constant_dynamic-update-slice_fusion, s32[]{:T(128)S(6)} %select_n.243), kind=kOutput, calls=%fused_computation.31 | convolution fusion | flops 536870912 | bytes 3670020 | tf_op jit(solution)/shard_map/dot_general | solution.py:147
  (78 shorter events, 6.4 us)
Async XLA Ops:
  12.1 1.8 copy-start.3
  16.2 8.1 %copy-start.5 = (s32[32]{0:T(128)S(1)}, s32[32]{0:T(128)}, u32[]{:S(2)}) copy-start(s32[32]{0:T(128)} %param.10) | copy-start | bytes 388
  16.2 9.6 %copy-start.4 = (s32[32,8]{0,1:T(8,128)S(1)}, s32[32,8]{0,1:T(8,128)}, u32[]{:S(2)}) copy-start(s32[32,8]{0,1:T(8,128)} %param.9) | copy-start | bytes 3076
  16.2 56.1 %all-to-all-start = ((bf16[32,2,128,128]{3,2,1,0:T(8,128)(2,1)}), bf16[32,2,128,128]{3,2,1,0:T(8,128)(2,1)S(1)}, u32[]{:S(2)}, u32[]{:S(2)}) async-start(bf16[32,2,128,128]{3,2,1,0:T(8,128)(2,1)} %copy.81), calls=%async_computation | async-start | bytes 4194304 | tf_op jit(solution)/shard_map/all_to_all | solution.py:78
  23.5 125.0 %all-gather.6.cloned.1.call-start = ((), (), s32[]{:S(2)}) async-start(), calls=%async_computation.3 | async-start | bytes 2359296 | tf_op jit(solution)/shard_map/all_gather | solution.py:143
  72.3 1.4 copy-start.1
  83.4 2.2 copy-start
  115.7 30.3 %all-to-all-start.1 = ((bf16[32,2,64,128]{3,2,1,0:T(8,128)(2,1)}), bf16[32,2,64,128]{3,2,1,0:T(8,128)(2,1)S(1)}, u32[]{:S(2)}, u32[]{:S(2)}) async-start(bf16[32,2,64,128]{3,2,1,0:T(8,128)(2,1)} %copy.86), calls=%async_computation.1 | async-start | bytes 2097152 | tf_op jit(solution)/shard_map/all_to_all | solution.py:117
  119.8 55.1 %all-gather.8.cloned.1.call-start = ((), (), s32[]{:S(2)}) async-start(), calls=%async_computation.4 | async-start | bytes 1310720 | tf_op jit(solution)/shard_map/all_gather | solution.py:140
  147.7 47.7 %copy-start.2 = (bf16[32,8,4,128]{3,1,2,0:T(8,128)(2,1)S(1)}, bf16[32,8,4,128]{3,1,2,0:T(8,128)(2,1)}, u32[]{:S(2)}) copy-start(bf16[32,8,4,128]{3,1,2,0:T(8,128)(2,1)} %copy.107) | copy-start | bytes 786436
  147.7 61.7 %all-gather.4.cloned.1.call-start = ((), (), s32[]{:S(2)}) async-start(), calls=%async_computation.2 | async-start | bytes 2359296 | tf_op jit(solution)/shard_map/all_gather | solution.py:148
  177.5 9.4 %collective-permute-start = (bf16[512,256]{1,0:T(8,128)(2,1)S(1)}, bf16[512,256]{1,0:T(8,128)(2,1)S(1)}, u32[]{:S(2)}, u32[]{:S(2)}) collective-permute-start(bf16[512,256]{1,0:T(8,128)(2,1)S(1)} %convolution_convert_fusion.2), channel_id=1, source_target_pairs={{0,8},{8,16},{16,24},{24,0},{1,9},{9,17},{17,25},{25,1},{2,10},{10... | collective-permute-start | bytes 786440 | tf_op jit(solution)/shard_map/ppermute | solution.py:16
  186.9 8.5 %collective-permute-start.1 = (bf16[512,256]{1,0:T(8,128)(2,1)S(1)}, bf16[512,256]{1,0:T(8,128)(2,1)S(1)}, u32[]{:S(2)}, u32[]{:S(2)}) collective-permute-start(bf16[512,256]{1,0:T(8,128)(2,1)S(1)} %collective-permute-done), channel_id=1, source_target_pairs={{0,8},{8,16},{16,24},{24,0},{1,9},{9,17},{17,25},{25,1},{2,10},{10... | collective-permute-start | bytes 786440 | tf_op jit(solution)/shard_map/ppermute | solution.py:16
  195.4 8.2 %collective-permute-start.2 = (bf16[512,256]{1,0:T(8,128)(2,1)S(1)}, bf16[512,256]{1,0:T(8,128)(2,1)S(1)}, u32[]{:S(2)}, u32[]{:S(2)}) collective-permute-start(bf16[512,256]{1,0:T(8,128)(2,1)S(1)} %collective-permute-done.1), channel_id=1, source_target_pairs={{0,8},{8,16},{16,24},{24,0},{1,9},{9,17},{17,25},{25,1},{2,10},{10... | collective-permute-start | bytes 786440 | tf_op jit(solution)/shard_map/ppermute | solution.py:16
Sparse Core Ops, SparseCore 0:
  26.8 35.3 all-gather.5
  147.8 26.9 all-gather.7
  177.3 27.1 all-gather.3
